TPU v7x, 32 devices: a whole 2x2x4 slice. The times are simulated.
32 devices in a mesh: fsdp: 32 (over z, y, x, core).
Axes of the slice: x: 2, y: 2, z: 4, core: 2. Of those that a mesh axis runs over, the one named last changes fastest.
Arguments:
- inputs: bfloat16 [32, 128, 768], P('fsdp'), may hold values from -6 to 6
- encoded: bfloat16 [32, 64, 768], P('fsdp')
- lengths: int32 [32], P('fsdp'), may hold values from 32 to 128, as said below
- bucket_ids: int32 [128], replicated, may hold values from 0 to 31, as said below
- qkv_weights: bfloat16 [768, 6, 768], P('fsdp')
- out_weights: bfloat16 [768, 2, 768], P('fsdp'), may hold values from -1.75 to 1.75
- ff_in: bfloat16 [768, 2, 2048], P('fsdp'), may hold values from -0.21875 to 0.21875
- ff_out: bfloat16 [2048, 768], P('fsdp'), may hold values from -0.125 to 0.125
- gains: bfloat16 [3, 768], P(None, 'fsdp'), may hold values from 0.5 to 1.5
- bias_table: float32 [32, 12], replicated
- cotangent: bfloat16 [32, 128, 768], P('fsdp'), may hold values from -6 to 6
Outputs:
- outputs: bfloat16 [32, 128, 768], P('fsdp')
- input_grad: bfloat16 [32, 128, 768], P('fsdp')
- encoded_grad: bfloat16 [32, 64, 768], P('fsdp')
- qkv_grad: float32 [768, 6, 768], P('fsdp')
- out_grad: float32 [768, 2, 768], P('fsdp')
- ffin_grad: float32 [768, 2, 2048], P('fsdp')
- ffout_grad: float32 [2048, 768], P('fsdp')
- gain_grad: float32 [3, 768], P(None, 'fsdp')
- table_grad: float32 [32, 12], replicated
Inputs may be any that keep to these rules, and one draw needn't show every extreme that they name: `lengths`: some sequence uses all 128 slots. `bucket_ids`: non-decreasing in the distance; distance 0 has bucket 0 and distance 128 - 1 bucket 32 - 1.
All inputs are finite; a program needn't handle non-finite values.
Results may differ from a plain program's by a relative error of at most 0.02.
Values may be sent and summed in bfloat16 or wider, within the bound.
A program may use at most 192 MiB of HBM per device.

v0:
```python
import jax
import jax.numpy as jnp
from jax import lax
from jax.sharding import PartitionSpec as P

HEAD = 64
EPS = 1e-06


def prod(form, left, right):
    return jnp.einsum(form, left, right, preferred_element_type=jnp.float32)


def gelu_tanh(value):
    return (
        0.5
        * value
        * (1.0 + jnp.tanh(0.7978845608028654 * (value + 0.044715 * value * value * value)))
    )


def rms_fwd(value, gain):
    recip = lax.rsqrt(jnp.mean(value * value, axis=-1, keepdims=True) + EPS)
    normed = value * recip
    return ((normed * gain).astype(jnp.bfloat16), normed, recip)


def rms_bwd(grad, normed, recip, gain):
    scaled = grad * gain
    gain_grad = jnp.sum(grad * normed, axis=0)
    back = recip * (scaled - normed * jnp.mean(scaled * normed, axis=-1, keepdims=True))
    return (back, gain_grad)


def toeplitz_bias(bucket_ids, table, positions):
    onehot = (bucket_ids[:, None] == jnp.arange(table.shape[0], dtype=jnp.int32)[None, :]).astype(
        jnp.float32
    )
    by_dist = jnp.transpose(jnp.dot(onehot, table, precision=lax.Precision.HIGHEST), (1, 0))
    head_count = by_dist.shape[0]
    nearest = jnp.broadcast_to(by_dist[:, 0:1], (head_count, positions))
    cyclic = jnp.concatenate(
        [nearest, jnp.zeros((head_count, 1), jnp.float32), by_dist[:, :0:-1]], axis=1
    )
    tiled = jnp.broadcast_to(cyclic[:, None, :], (head_count, positions, 2 * positions))
    tiled = tiled.reshape(head_count, 2 * positions * positions)
    skewed = tiled[:, : positions * (2 * positions - 1)].reshape(
        head_count, positions, 2 * positions - 1
    )
    return (skewed[:, :, :positions], onehot)


def diagonal_sums(d_score, onehot):
    head_count, positions = (d_score.shape[0], d_score.shape[1])
    padded = jnp.pad(d_score, ((0, 0), (0, 0), (0, positions - 1)))
    padded = padded.reshape(head_count, positions * (2 * positions - 1))
    padded = jnp.pad(padded, ((0, 0), (0, positions))).reshape(head_count, positions, 2 * positions)
    column = jnp.sum(padded, axis=1)
    by_dist = jnp.concatenate(
        [jnp.sum(column[:, :positions], axis=1, keepdims=True), column[:, :positions:-1]], axis=1
    )
    return jnp.dot(
        jnp.transpose(onehot, (1, 0)),
        jnp.transpose(by_dist, (1, 0)),
        precision=lax.Precision.HIGHEST,
    )


def scores_of(query, keys, bias, mask):
    rows = query.shape[0]
    q3 = query.reshape(rows, -1, HEAD)
    k3 = keys.reshape(keys.shape[0], -1, HEAD)
    scores = prod("qhd,khd->hqk", q3, k3)
    if bias is not None:
        scores = scores + bias
    if mask is not None:
        scores = jnp.where(mask[None], scores, -1e30)
    return scores


def attend(query, keys, values, bias, mask, shifted):
    rows = query.shape[0]
    scores = scores_of(query, keys, bias, mask)
    if shifted:
        top = jnp.max(scores, axis=-1, keepdims=True)
        lse = top + jnp.log(jnp.sum(jnp.exp(scores - top), axis=-1, keepdims=True))
    else:
        lse = jnp.log(jnp.sum(jnp.exp(scores), axis=-1, keepdims=True))
    prob = jnp.exp(scores - lse).astype(jnp.bfloat16)
    v3 = values.reshape(values.shape[0], -1, HEAD)
    out = prod("hqk,khd->qhd", prob, v3).reshape(rows, -1).astype(jnp.bfloat16)
    return (out, lse)


def attend_back(query, keys, values, out, lse, grad_out, bias, mask):
    rows = query.shape[0]
    scores = scores_of(query, keys, bias, mask)
    prob = jnp.exp(scores - lse)
    prob_b = prob.astype(jnp.bfloat16)
    q3 = query.reshape(rows, -1, HEAD)
    k3 = keys.reshape(keys.shape[0], -1, HEAD)
    v3 = values.reshape(values.shape[0], -1, HEAD)
    grad3 = grad_out.reshape(rows, -1, HEAD)
    grad_b = grad3.astype(jnp.bfloat16)
    out3 = out.reshape(rows, -1, HEAD).astype(jnp.float32)
    d_val = prod("hqk,qhd->khd", prob_b, grad_b)
    d_prob = prod("qhd,khd->hqk", grad_b, v3)
    delta = jnp.transpose(jnp.sum(grad3 * out3, axis=2), (1, 0))
    d_score = prob * (d_prob - delta[:, :, None])
    d_score_b = d_score.astype(jnp.bfloat16)
    d_query = prod("hqk,khd->qhd", d_score_b, k3)
    d_key = prod("hqk,qhd->khd", d_score_b, q3)
    shape_q = (rows, -1)
    shape_k = (keys.shape[0], -1)
    return (
        d_query.reshape(shape_q).astype(jnp.bfloat16),
        d_key.reshape(shape_k).astype(jnp.bfloat16),
        d_val.reshape(shape_k).astype(jnp.bfloat16),
        d_score,
    )


def forward(rows, enc, length, bucket_ids, weights, table):
    qkv_w, out_w, ff_in, ff_out, gains = weights
    positions = rows.shape[0]
    gain_f = gains.astype(jnp.float32)
    start = rows.astype(jnp.float32)
    h1, n1, r1 = rms_fwd(start, gain_f[0])
    qkv = prod("ld,cde->cle", h1, qkv_w[0:3]).astype(jnp.bfloat16)
    row_ids = lax.broadcasted_iota(jnp.int32, (positions, positions), 0)
    col_ids = lax.broadcasted_iota(jnp.int32, (positions, positions), 1)
    mask = (col_ids <= row_ids) & (col_ids < length)
    bias, onehot = toeplitz_bias(bucket_ids, table, positions)
    a1, lse1 = attend(qkv[0], qkv[1], qkv[2], bias, mask, True)
    x1 = start + prod("le,ed->ld", a1, out_w[0])
    h2, n2, r2 = rms_fwd(x1, gain_f[1])
    qc = prod("ld,de->le", h2, qkv_w[3]).astype(jnp.bfloat16)
    kvc = prod("ld,cde->cle", enc, qkv_w[4:6]).astype(jnp.bfloat16)
    ac, lse2 = attend(qc, kvc[0], kvc[1], None, None, False)
    x2 = x1 + prod("le,ed->ld", ac, out_w[1])
    h3, n3, r3 = rms_fwd(x2, gain_f[2])
    gate_up = prod("ld,cdf->clf", h3, ff_in)
    hidden = (gelu_tanh(gate_up[0]) * gate_up[1]).astype(jnp.bfloat16)
    result = x2 + prod("lf,fd->ld", hidden, ff_out)
    saved = (
        h1,
        n1,
        r1,
        qkv,
        bias,
        mask,
        a1,
        lse1,
        h2,
        n2,
        r2,
        qc,
        kvc,
        ac,
        lse2,
        h3,
        n3,
        r3,
        gate_up,
        hidden,
        onehot,
    )
    return (result.astype(jnp.bfloat16), saved)


def ff_back(saved, weights, cot):
    qkv_w, out_w, ff_in, ff_out, gains = weights
    gain_f = gains.astype(jnp.float32)
    h3, n3, r3, gate_up, hidden = (saved[15], saved[16], saved[17], saved[18], saved[19])
    d_ffout = prod("lf,ld->fd", hidden, cot)
    d_hidden = prod("ld,fd->lf", cot, ff_out)
    gelu_val, gelu_pull = jax.vjp(gelu_tanh, gate_up[0])
    d_gate = gelu_pull(d_hidden * gate_up[1])[0]
    d_up = d_hidden * gelu_val
    d_gate_up = jnp.stack([d_gate, d_up]).astype(jnp.bfloat16)
    d_ffin = prod("ld,clf->cdf", h3, d_gate_up)
    d_h3 = prod("clf,cdf->ld", d_gate_up, ff_in)
    back3, gain3 = rms_bwd(d_h3, n3, r3, gain_f[2])
    return (cot.astype(jnp.float32) + back3, d_ffin, d_ffout, gain3)


def cross_back(saved, weights, enc, dx2):
    qkv_w, out_w, ff_in, ff_out, gains = weights
    gain_f = gains.astype(jnp.float32)
    h2, n2, r2, qc, kvc, ac, lse2 = (
        saved[8],
        saved[9],
        saved[10],
        saved[11],
        saved[12],
        saved[13],
        saved[14],
    )
    dx2_b = dx2.astype(jnp.bfloat16)
    d_outc = prod("le,ld->ed", ac, dx2_b)
    d_ac = prod("ld,ed->le", dx2_b, out_w[1])
    d_qc, d_kc, d_vc, unused = attend_back(qc, kvc[0], kvc[1], ac, lse2, d_ac, None, None)
    g_qc = prod("ld,le->de", h2, d_qc)
    d_kvc = jnp.stack([d_kc, d_vc])
    g_kvc = prod("ld,cle->cde", enc, d_kvc)
    enc_grad = prod("cle,cde->ld", d_kvc, qkv_w[4:6]).astype(jnp.bfloat16)
    d_h2 = prod("le,de->ld", d_qc, qkv_w[3])
    back2, gain2 = rms_bwd(d_h2, n2, r2, gain_f[1])
    return (dx2 + back2, g_qc, g_kvc, d_outc, gain2, enc_grad)


def self_back(saved, weights, dx1):
    qkv_w, out_w, ff_in, ff_out, gains = weights
    gain_f = gains.astype(jnp.float32)
    h1, n1, r1, qkv, bias, mask, a1, lse1 = saved[0:8]
    onehot = saved[20]
    dx1_b = dx1.astype(jnp.bfloat16)
    d_outs = prod("le,ld->ed", a1, dx1_b)
    d_a1 = prod("ld,ed->le", dx1_b, out_w[0])
    d_q, d_k, d_v, d_score = attend_back(qkv[0], qkv[1], qkv[2], a1, lse1, d_a1, bias, mask)
    d_qkv = jnp.stack([d_q, d_k, d_v])
    g_qkv = prod("ld,cle->cde", h1, d_qkv)
    d_h1 = prod("cle,cde->ld", d_qkv, qkv_w[0:3])
    back1, gain1 = rms_bwd(d_h1, n1, r1, gain_f[0])
    d_table = diagonal_sums(d_score, onehot)
    return ((dx1 + back1).astype(jnp.bfloat16), g_qkv, d_outs, gain1, d_table)


def to_blocks(array, width):
    blocks = []
    for copy in range(array.shape[0]):
        for start in range(0, array.shape[-1], width):
            block = array[copy, ..., start : start + width]
            short = width - block.shape[-1]
            if short:
                block = jnp.pad(block, ((0, 0),) * (block.ndim - 1) + ((0, short),))
            blocks.append(block)
    return blocks


def from_blocks(blocks, shape, width):
    copies, rows, columns = shape
    each = -(-columns // width)
    planes = []
    for copy in range(copies):
        part = [blocks[copy * each + at] for at in range(each)]
        part[-1] = part[-1][..., : columns - (each - 1) * width]
        planes.append(part[0] if each == 1 else jnp.concatenate(part, axis=-1))
    return planes


def per_device(
    inputs,
    encoded,
    lengths,
    bucket_ids,
    qkv_weights,
    out_weights,
    ff_in,
    ff_out,
    gains,
    bias_table,
    cotangent,
):
    count = lax.axis_size("fsdp")
    shards = (
        jnp.transpose(qkv_weights, (1, 0, 2)),
        jnp.transpose(out_weights, (1, 0, 2)),
        jnp.transpose(ff_in, (1, 0, 2)),
        ff_out[None],
    )
    width = qkv_weights.shape[-1]
    depth = qkv_weights.shape[0]
    tall = ff_out.shape[0]
    blocks = to_blocks(shards[0], width) + to_blocks(shards[1], width) + to_blocks(shards[2], width)
    slots = gains.size
    tail = 8 * -(-slots // (8 * width))
    gain_rows = jnp.pad(gains.reshape(1, slots), ((0, 0), (0, tail * width - slots)))
    packed = jnp.concatenate(blocks + [ff_out, gain_rows.reshape(tail, width)], axis=0)
    whole = lax.all_gather(packed, "fsdp", axis=0, tiled=False)
    cut = len(blocks) * depth
    stacked = whole[:, :cut].reshape(count, len(blocks), depth, width)
    stacked = jnp.transpose(stacked, (1, 0, 2, 3)).reshape(len(blocks), count * depth, width)
    ff_out_all = whole[:, cut : cut + tall].reshape(count * tall, width)
    stacked, ff_out_all = lax.optimization_barrier((stacked, ff_out_all))
    n_qkv, n_out = (qkv_weights.shape[1], out_weights.shape[1])
    ff_all = jnp.stack(from_blocks(stacked[n_qkv + n_out :], shards[2].shape, width))
    main = (stacked[:n_qkv], stacked[n_qkv : n_qkv + n_out], ff_all, ff_out_all[None])
    gain_all = whole[:, -tail:].reshape(count, tail * width)[:, :slots]
    gain_all = gain_all.reshape(count, gains.shape[0], gains.shape[1])
    gain_all = jnp.transpose(gain_all, (1, 0, 2)).reshape(gains.shape[0], -1)
    weights = (main[0], main[1], main[2], main[3][0], gain_all)
    result, saved = forward(inputs[0], encoded[0], lengths[0], bucket_ids, weights, bias_table)
    dx2, g_ffin, g_ffout, gain3 = ff_back(saved, weights, cotangent[0])
    dx1, g_qc, g_kvc, g_outc, gain2, enc_grad = cross_back(saved, weights, encoded[0], dx2)
    dx, g_qkvs, g_outs, gain1, g_table = self_back(saved, weights, dx1)
    wide = [g_qkvs[0], g_qkvs[1], g_qkvs[2], g_qc, g_kvc[0], g_kvc[1], g_outs, g_outc]
    wide += to_blocks(g_ffin, width)
    wide.append(g_ffout)
    g_gain = jnp.stack([gain1, gain2, gain3]).reshape(gains.shape[0], count, -1)
    g_gain = jnp.transpose(g_gain, (1, 0, 2)).reshape(count, slots)
    g_gain = jnp.pad(g_gain, ((0, 0), (0, tail * width - slots))).reshape(count, tail, width)
    parts = [grad.astype(jnp.bfloat16).reshape(count, -1, width) for grad in wide]
    send = jnp.concatenate(parts + [g_gain.astype(jnp.bfloat16)], axis=1)
    send, g_table = lax.optimization_barrier((send, g_table))
    own = lax.psum_scatter(send, "fsdp", scatter_dimension=0, tiled=False).astype(jnp.float32)
    mine = own[:cut].reshape(len(blocks), depth, width)
    s_ffin = jnp.stack(from_blocks(mine[n_qkv + n_out :], shards[2].shape, width))
    s_main = (mine[:n_qkv], mine[n_qkv : n_qkv + n_out], s_ffin, own[cut : cut + tall][None])
    s_gain = own[-tail:].reshape(tail * width)[:slots].reshape(gains.shape)
    s_table = lax.psum(g_table, "fsdp")
    return (
        result[None],
        dx[None],
        enc_grad[None],
        jnp.transpose(s_main[0], (1, 0, 2)),
        jnp.transpose(s_main[1], (1, 0, 2)),
        jnp.transpose(s_main[2], (1, 0, 2)),
        s_main[3][0],
        s_gain,
        s_table,
    )


def solution(mesh):
    placed = (
        P("fsdp", None, None),
        P("fsdp", None, None),
        P("fsdp"),
        P(),
        P("fsdp", None, None),
        P("fsdp", None, None),
        P("fsdp", None, None),
        P("fsdp", None),
        P(None, "fsdp"),
        P(),
        P("fsdp", None, None),
    )
    return jax.shard_map(
        per_device,
        mesh=mesh,
        in_specs=placed,
        out_specs=(
            P("fsdp", None, None),
            P("fsdp", None, None),
            P("fsdp", None, None),
            P("fsdp", None, None),
            P("fsdp", None, None),
            P("fsdp", None, None),
            P("fsdp", None),
            P(None, "fsdp"),
            P(),
        ),
        check_vma=False,
    )
```

profile of v0, /device:TPU:0, one launch (start us, length us, event | category | flops | bytes accessed | tf_op | source)
XLA Modules:
  0.0 536.2 jit_solution(1657681668492004055)
XLA Ops:
  18.3 1.2 copy.152
  19.7 3.4 reshape.321
  23.1 1.2 slice.401
  25.4 123.4 %all-gather.3.cloned.1.call-done = bf16[13056,768]{1,0:T(8,128)(2,1)} async-done(((bf16[408,768]{1,0:T(8,128)(2,1)}), bf16[13056,768]{1,0:T(8,128)(2,1)}) %all-gather.3.cloned.1.call-update) | async-done | bytes 20054032 | tf_op jit(solution)/shard_map/all_gather | solution.py:280
  148.8 7.9 %slice.390 = bf16[32,336,768]{2,1,0:T(8,128)(2,1)S(1)} slice(bf16[32,408,768]{2,1,0:T(8,128)(2,1)} %bitcast.363), slice={[0:32], [0:336], [0:768]} | slice | bytes 33030144 | tf_op jit(solution)/shard_map/slice | solution.py:282
  156.8 3.9 slice.391
  161.7 6.6 %copy.95 = bf16[14,32,24,768]{3,2,1,0:T(8,128)(2,1)} copy(bf16[14,32,24,768]{3,2,0,1:T(8,128)(2,1)S(1)} %bitcast.362) | data formatting | bytes 33030144 | tf_op jit(solution)/shard_map/transpose | solution.py:283
  168.3 22.3 %copy.96 = bf16[14,768,768]{1,2,0:T(8,128)(2,1)} copy(bf16[14,768,768]{2,1,0:T(8,128)(2,1)} %bitcast.353) | data formatting | bytes 33030144 | tf_op jit(solution)/shard_map/optimization_barrier | solution.py:285
  190.6 3.2 fusion.154
  194.8 3.2 fusion.12
  198.9 1.8 multiply_reduce_fusion.7
  200.7 2.2 fusion.35
  203.5 1.6 fusion.28
  207.4 1.7 multiply_reduce_fusion.6
  209.2 5.2 slice_bitcast_fusion.5
  216.4 3.0 maximum_bitcast_fusion
  219.4 1.9 fusion.5
  221.3 1.6 fusion.77
  223.0 1.8 multiply_reduce_fusion
  226.7 2.6 multiply_reduce_fusion.1
  231.9 2.1 convolution_convert_fusion.5
  235.3 4.0 fusion.84
  239.3 2.9 convert_bitcast_fusion.1
  242.3 1.6 convolution_convert_fusion.3
  243.9 1.5 convolution_convert_fusion.2
  245.4 1.5 convolution_convert_fusion.1
  246.8 2.1 convert_bitcast_fusion
  249.0 2.2 fusion.155
  251.2 1.4 slice_bitcast_fusion.6
  254.6 2.3 copy.150
  256.9 2.5 pad.39.clone
  259.3 3.9 reshape.330
  263.2 1.7 pad.40
  267.4 1.7 copy.124
  269.1 3.7 fusion.156
  272.8 1.1 constant_dynamic-update-slice_fusion.31
  274.8 1.6 fusion.157
  276.4 1.1 pad.36
  278.6 1.4 stack.63
  280.0 1.4 stack.62
  281.3 1.4 stack.61
  282.7 1.3 maximum_bitcast_fusion.5
  284.1 1.4 copy.129
  285.5 2.1 pad.38
  287.6 2.4 copy.130
  290.7 1.3 copy.132
  292.0 2.5 constant_dynamic-update-slice_fusion.30
  294.6 1.1 constant_dynamic-update-slice_fusion.29
  295.7 1.1 constant_dynamic-update-slice_fusion.28
  296.8 1.1 constant_dynamic-update-slice_fusion.27
  298.0 1.2 constant_dynamic-update-slice_fusion.26
  300.2 1.1 constant_dynamic-update-slice_fusion.24
  301.4 1.1 constant_dynamic-update-slice_fusion.23
  302.5 1.1 constant_dynamic-update-slice_fusion.22
  303.6 1.1 constant_dynamic-update-slice_fusion.21
  304.8 1.1 constant_dynamic-update-slice_fusion.20
  307.0 1.2 constant_dynamic-update-slice_fusion.18
  308.2 1.9 constant_dynamic-update-slice_fusion.17
  311.9 38.4 %psum.7 = f32[32,12]{0,1:T(8,128)} all-reduce(f32[32,12]{0,1:T(8,128)S(1)} %fusion.123), channel_id=1, replica_groups=mesh['fsdp'=32] {'fsdp'}, use_global_device_ids=true, to_apply=%region_17.18 | all-reduce | flops 384 | bytes 3072 | tf_op jit(solution)/shard_map/psum | solution.py:311
  350.3 3.5 fusion.45
  353.8 1.9 fusion.89
  355.7 1.5 fusion.41
  357.2 166.7 %reduce-scatter.2.cloned.1.call-done = bf16[1,408,768]{2,1,0:T(8,128)(2,1)} async-done(((bf16[32,408,768]{2,1,0:T(8,128)(2,1)}), bf16[1,408,768]{2,1,0:T(8,128)(2,1)}) %reduce-scatter.2.cloned.1.call-update) | async-done | bytes 626704 | tf_op jit(solution)/shard_map/reduce_scatter | solution.py:306
  523.9 1.3 fusion.159
  (247 shorter events, 40.1 us)
Async XLA Ops:
  7.2 193.5 %copy-start = (bf16[1,64,768]{2,1,0:T(8,128)(2,1)S(1)}, bf16[1,64,768]{2,1,0:T(8,128)(2,1)}, u32[]{:S(2)}) copy-start(bf16[1,64,768]{2,1,0:T(8,128)(2,1)} %param.12) | copy-start | bytes 294916
  7.2 141.7 %all-gather.3.cloned.1.call-start = ((), (), s32[]{:S(2)}) async-start(), calls=%async_computation.2 | async-start | bytes 20680704 | tf_op jit(solution)/shard_map/all_gather | solution.py:280
  16.5 507.4 %reduce-scatter.2.cloned.1.call-start = ((), (), s32[]{:S(2)}) async-start(), calls=%async_computation.1 | async-start | bytes 20680704 | tf_op jit(solution)/shard_map/reduce_scatter | solution.py:306
  19.7 5.5 %copy-start.4 = (bf16[1,128,768]{2,1,0:T(8,128)(2,1)S(1)}, bf16[1,128,768]{2,1,0:T(8,128)(2,1)}, u32[]{:S(2)}) copy-start(bf16[1,128,768]{2,1,0:T(8,128)(2,1)} %param.11) | copy-start | bytes 589828
  198.1 4.8 copy-start.34
  198.1 4.8 copy-start.36
  198.1 4.8 copy-start.38
  198.8 6.2 %copy-start.26 = (bf16[12,64,128]{2,1,0:T(8,128)(2,1)}, bf16[12,64,128]{2,1,0:T(8,128)(2,1)S(1)}, u32[]{:S(2)}) copy-start(bf16[12,64,128]{2,1,0:T(8,128)(2,1)S(1)} %convolution_convert_fusion.12) | copy-start | bytes 589828
  203.1 3.7 copy-start.48
  203.3 3.5 copy-start.32
  205.3 1.5 copy-start.30
  209.1 15.7 %copy-start.19 = (f32[128,768]{1,0:T(8,128)}, f32[128,768]{1,0:T(8,128)S(1)}, u32[]{:S(2)}) copy-start(f32[128,768]{1,0:T(8,128)S(1)} %get-tuple-element.94) | copy-start | bytes 1179652
  219.4 1.9 copy-start.22
  219.4 1.9 copy-start.50
  221.3 1.6 copy-start.61
  223.0 1.9 copy-start.57
  223.0 1.9 copy-start.59
  223.0 2.1 copy-start.18
  223.0 2.1 copy-start.41
  224.8 1.4 copy-start.46
  224.8 1.4 copy-start.49
  224.8 1.6 copy-start.33
  225.6 3.9 copy-start.17
  225.6 3.9 copy-start.27
  226.4 2.8 copy-start.43
  226.7 2.6 copy-start.52
  226.7 3.7 copy-start.39
  229.3 1.4 copy-start.37
  229.4 14.5 %copy-start.2 = (f32[128,768]{1,0:T(8,128)}, f32[128,768]{1,0:T(8,128)S(1)}, u32[]{:S(2)}) copy-start(f32[128,768]{1,0:T(8,128)S(1)} %multiply_add_fusion.3) | copy-start | bytes 1179652
  229.5 2.2 copy-start.35
  229.9 1.9 copy-start.55
  230.0 4.0 copy-start.31
  230.0 4.0 copy-start.44
  239.3 3.0 copy-start.53
  239.3 4.5 copy-start.28
  239.3 6.0 %copy-start.42 = (bf16[12,64,128]{2,1,0:T(8,128)(2,1)S(1)}, bf16[12,64,128]{2,1,0:T(8,128)(2,1)}, u32[]{:S(2)}) copy-start(bf16[12,64,128]{2,1,0:T(8,128)(2,1)} %copy-done.40) | copy-start | bytes 589828
  242.3 4.6 copy-start.20
  242.3 4.6 copy-start.58
  242.3 4.6 copy-start.60
  251.2 2.3 copy-start.62
  269.1 4.8 copy-start.64
  274.0 2.4 copy-start.25
  274.8 2.7 copy-start.24
  292.0 2.5 copy-start.9
  292.0 3.6 copy-start.12
  292.0 4.8 copy-start.16
  294.5 3.4 copy-start.15
  295.7 3.5 copy-start.11
  296.8 3.4 copy-start.10
  298.0 3.4 copy-start.8
  299.1 3.4 copy-start.7
  300.2 3.4 copy-start.14
  301.4 3.4 copy-start.6
  302.5 3.4 copy-start.5
  303.6 3.4 copy-start.13
  308.2 1.9 copy-start.47
  308.2 2.7 copy-start.66
  311.8 38.5 %copy-start.67 = (f32[128]{0:T(128)S(1)}, f32[128]{0:T(128)}, u32[]{:S(2)}) copy-start(f32[128]{0:T(128)} %get-tuple-element.49) | copy-start | bytes 1540
  311.8 38.5 %copy-start.65 = (bf16[1,64,768]{2,1,0:T(8,128)(2,1)S(1)}, bf16[1,64,768]{2,1,0:T(8,128)(2,1)}, u32[]{:S(2)}) copy-start(bf16[1,64,768]{2,1,0:T(8,128)(2,1)} %copy.124) | copy-start | bytes 294916
  311.8 43.9 %copy-start.63 = (f32[2,128,2048]{1,2,0:T(8,128)S(1)}, f32[2,128,2048]{1,2,0:T(8,128)}, u32[]{:S(2)}) copy-start(f32[2,128,2048]{1,2,0:T(8,128)} %copy-done.61) | copy-start | bytes 6291460
  311.9 41.9 %copy-start.3 = (f32[128,768]{1,0:T(8,128)S(1)}, f32[128,768]{1,0:T(8,128)}, u32[]{:S(2)}) copy-start(f32[128,768]{1,0:T(8,128)} %copy-done.2) | copy-start | bytes 1179652
  311.9 43.8 %copy-start.21 = (f32[128,768]{1,0:T(8,128)S(1)}, f32[128,768]{1,0:T(8,128)}, u32[]{:S(2)}) copy-start(f32[128,768]{1,0:T(8,128)} %copy-done.19) | copy-start | bytes 1179652
  350.3 5.4 %copy-start.23 = (bf16[32,64,768]{2,1,0:T(8,128)(2,1)S(1)}, bf16[32,64,768]{2,1,0:T(8,128)(2,1)}, u32[]{:S(2)}) copy-start(bf16[32,64,768]{2,1,0:T(8,128)(2,1)} %slice.391) | copy-start | bytes 9437188
  523.9 2.0 copy-start.29
  (6 other events, 5.8 us)
Sparse Core Ops, SparseCore 0:
  16.6 132.1 all-gather.2
  312.0 211.8 reduce-scatter.1
where the time goes:
time: 538 us; the launch traced here: 536 us
  waiting for transfers between devices  290 us (54%)
  local copies, waits for them, and re-layouts  134 us (25%)
  matrix products  47.5 us (9%)
  blocking collectives  38.4 us (7%)
  between operations  15.8 us (3%)
  other arithmetic  10 us (2%)
    reduce_scatter x1, waiting for transfers between devices, per_device(): lax.psum_scatter(send, 'fsdp', scatter_dimension=0, tiled=False)  167 us
    all_gather x1, waiting for transfers between devices, per_device(): whole = lax.all_gather(packed, 'fsdp', axis=0, tiled=False)  123 us
    dot_general x33, matrix products, prod(): return jnp.einsum(form, left, right, preferred_element_type=jnp.float32)  45.6 us
    psum x1, blocking collectives, per_device(): s_table = lax.psum(g_table, 'fsdp')  38.4 us
    unnamed x174, local copies, waits for them, and re-layouts  36.2 us
    optimization_barrier x1, local copies, waits for them, and re-layouts, per_device(): stacked, ff_out_all = lax.optimization_barrier((stacked, ff_out_all))  22.3 us
  transfers between devices with their start and end apart: 2, of which 2 were waited for; matrix products, arithmetic and copies ran while one was open for 3% of the time, Pallas kernels for 0%

commit v1 on v0

--- a/solution.py
+++ b/solution.py
@@ -5,6 +5,23 @@
 
 HEAD = 64
 EPS = 1e-06
+
+
+def streams_rest(named_axis, matrix):
+    sides = lax.axis_size(named_axis)
+
+    def detail_leaves(value_now, long_array):
+        if long_array >= sides:
+            return value_now
+        return detail_leaves(
+            value_now
+            + lax.ppermute(
+                value_now, named_axis, list(map(lambda j0: (j0, j0 ^ long_array), range(sides)))
+            ),
+            2 * long_array,
+        )
+
+    return detail_leaves(matrix, 1)
 
 
 def prod(form, left, right):
@@ -308,7 +325,7 @@
     s_ffin = jnp.stack(from_blocks(mine[n_qkv + n_out :], shards[2].shape, width))
     s_main = (mine[:n_qkv], mine[n_qkv : n_qkv + n_out], s_ffin, own[cut : cut + tall][None])
     s_gain = own[-tail:].reshape(tail * width)[:slots].reshape(gains.shape)
-    s_table = lax.psum(g_table, "fsdp")
+    s_table = streams_rest("fsdp", g_table)
     return (
         result[None],
         dx[None],

time: 538 us -> 539 us (level)
  blocking collectives: 38.4 us -> 0 us
  waiting for transfers between devices: 290 us -> 324 us
    psum x1 -> x0, blocking collectives: 38.4 us -> none  [per_device(): s_table = lax.psum(g_table, 'fsdp')]
    reduce_scatter x1, waiting for transfers between devices: 167 us -> 193 us  [per_device(): lax.psum_scatter(send, 'fsdp', scatter_dimension=0, tiled=False)]
    ppermute x0 -> x5, waiting for transfers between devices: none -> 7.24 us  [detail_leaves(): lax.ppermute(value_now, named_axis, list(map(lambda j0: (j0, j0 ^ long_ar...]
  transfers between devices with their start and end apart: 2 -> 7, of which waited for: 2 -> 6; matrix products, arithmetic and copies ran while one was open for 3% -> 3% of each run, Pallas kernels for 0% -> 0%
where the time goes in v1:
time: 539 us; the launch traced here: 536 us
  waiting for transfers between devices  324 us (60%)
  local copies, waits for them, and re-layouts  134 us (25%)
  matrix products  49.6 us (9%)
  between operations  15.8 us (3%)
  other arithmetic  9.61 us (2%)
    reduce_scatter x1, waiting for transfers between devices, per_device(): lax.psum_scatter(send, 'fsdp', scatter_dimension=0, tiled=False)  193 us
    all_gather x1, waiting for transfers between devices, per_device(): whole = lax.all_gather(packed, 'fsdp', axis=0, tiled=False)  123 us
    dot_general x33, matrix products, prod(): return jnp.einsum(form, left, right, preferred_element_type=jnp.float32)  47.8 us
    unnamed x174, local copies, waits for them, and re-layouts  36.3 us
    optimization_barrier x1, local copies, waits for them, and re-layouts, per_device(): stacked, ff_out_all = lax.optimization_barrier((stacked, ff_out_all))  22.3 us
  transfers between devices with their start and end apart: 7, of which 6 were waited for; matrix products, arithmetic and copies ran while one was open for 3% of the time, Pallas kernels for 0%

profile of v1, /device:TPU:0, one launch (start us, length us, event | category | flops | bytes accessed | tf_op | source)
XLA Modules:
  0.0 536.3 jit_solution(10097828467222876438)
XLA Ops:
  18.3 1.2 copy.152
  19.7 3.4 reshape.321
  23.1 1.2 slice.401
  25.4 123.4 %all-gather.3.cloned.1.call-done = bf16[13056,768]{1,0:T(8,128)(2,1)} async-done(((bf16[408,768]{1,0:T(8,128)(2,1)}), bf16[13056,768]{1,0:T(8,128)(2,1)}) %all-gather.3.cloned.1.call-update) | async-done | bytes 20054032 | tf_op jit(solution)/shard_map/all_gather | solution.py:297
  148.8 7.9 %slice.390 = bf16[32,336,768]{2,1,0:T(8,128)(2,1)S(1)} slice(bf16[32,408,768]{2,1,0:T(8,128)(2,1)} %bitcast.363), slice={[0:32], [0:336], [0:768]} | slice | bytes 33030144 | tf_op jit(solution)/shard_map/slice | solution.py:299
  156.8 3.9 slice.391
  161.7 6.6 %copy.95 = bf16[14,32,24,768]{3,2,1,0:T(8,128)(2,1)} copy(bf16[14,32,24,768]{3,2,0,1:T(8,128)(2,1)S(1)} %bitcast.362) | data formatting | bytes 33030144 | tf_op jit(solution)/shard_map/transpose | solution.py:300
  168.2 22.3 %copy.96 = bf16[14,768,768]{1,2,0:T(8,128)(2,1)} copy(bf16[14,768,768]{2,1,0:T(8,128)(2,1)} %bitcast.353) | data formatting | bytes 33030144 | tf_op jit(solution)/shard_map/optimization_barrier | solution.py:302
  190.5 3.2 fusion.154
  194.8 3.2 fusion.12
  198.8 1.8 multiply_reduce_fusion.7
  200.6 2.2 fusion.35
  203.4 1.6 fusion.28
  207.4 1.7 multiply_reduce_fusion.6
  209.1 5.1 slice_bitcast_fusion.5
  216.4 3.0 maximum_bitcast_fusion
  219.4 1.9 fusion.5
  221.3 1.6 fusion.77
  223.0 1.8 multiply_reduce_fusion
  226.6 2.6 multiply_reduce_fusion.1
  231.8 2.1 convolution_convert_fusion.5
  235.3 4.0 fusion.84
  239.3 2.9 convert_bitcast_fusion.1
  242.2 1.6 convolution_convert_fusion.3
  243.8 1.5 convolution_convert_fusion.2
  245.3 1.5 convolution_convert_fusion.1
  246.8 2.1 convert_bitcast_fusion
  248.9 2.2 fusion.155
  251.2 1.4 slice_bitcast_fusion.6
  254.5 2.3 copy.150
  256.8 2.4 pad.39.clone
  259.3 3.9 reshape.330
  263.1 1.7 pad.40
  267.3 1.7 copy.124
  269.0 3.7 fusion.156
  272.7 1.2 constant_dynamic-update-slice_fusion.31
  274.7 1.5 fusion.157
  276.3 1.1 pad.36
  278.5 1.4 stack.63
  279.9 1.4 stack.62
  281.3 1.4 stack.61
  282.7 1.3 maximum_bitcast_fusion.5
  284.0 1.4 copy.129
  285.4 2.1 pad.38
  287.5 2.4 copy.130
  290.6 1.3 copy.132
  292.0 2.5 constant_dynamic-update-slice_fusion.30
  295.6 1.1 constant_dynamic-update-slice_fusion.28
  296.7 1.2 constant_dynamic-update-slice_fusion.27
  297.9 1.1 constant_dynamic-update-slice_fusion.26
  299.1 1.1 constant_dynamic-update-slice_fusion.25
  300.2 1.2 constant_dynamic-update-slice_fusion.24
  301.4 1.2 constant_dynamic-update-slice_fusion.23
  302.5 1.2 constant_dynamic-update-slice_fusion.22
  304.8 1.1 constant_dynamic-update-slice_fusion.20
  306.0 1.1 constant_dynamic-update-slice_fusion.19
  308.2 1.9 constant_dynamic-update-slice_fusion.17
  313.3 1.4 collective-permute-start.1
  314.7 3.8 fusion.41
  318.7 3.4 collective-permute-done.2
  323.0 2.7 collective-permute-done.3
  326.9 3.3 fusion.45
  330.9 193.1 %reduce-scatter.2.cloned.1.call-done = bf16[1,408,768]{2,1,0:T(8,128)(2,1)} async-done(((bf16[32,408,768]{2,1,0:T(8,128)(2,1)}), bf16[1,408,768]{2,1,0:T(8,128)(2,1)}) %reduce-scatter.2.cloned.1.call-update) | async-done | bytes 626704 | tf_op jit(solution)/shard_map/reduce_scatter | solution.py:323
  524.0 1.3 fusion.159
  (261 shorter events, 45.4 us)
Async XLA Ops:
  7.2 193.4 %copy-start = (bf16[1,64,768]{2,1,0:T(8,128)(2,1)S(1)}, bf16[1,64,768]{2,1,0:T(8,128)(2,1)}, u32[]{:S(2)}) copy-start(bf16[1,64,768]{2,1,0:T(8,128)(2,1)} %param.12) | copy-start | bytes 294916
  7.2 141.7 %all-gather.3.cloned.1.call-start = ((), (), s32[]{:S(2)}) async-start(), calls=%async_computation.2 | async-start | bytes 20680704 | tf_op jit(solution)/shard_map/all_gather | solution.py:297
  16.5 507.5 %reduce-scatter.2.cloned.1.call-start = ((), (), s32[]{:S(2)}) async-start(), calls=%async_computation.1 | async-start | bytes 20680704 | tf_op jit(solution)/shard_map/reduce_scatter | solution.py:323
  19.7 5.5 %copy-start.4 = (bf16[1,128,768]{2,1,0:T(8,128)(2,1)S(1)}, bf16[1,128,768]{2,1,0:T(8,128)(2,1)}, u32[]{:S(2)}) copy-start(bf16[1,128,768]{2,1,0:T(8,128)(2,1)} %param.11) | copy-start | bytes 589828
  198.0 4.8 copy-start.33
  198.1 4.8 copy-start.35
  198.1 4.8 copy-start.37
  198.8 6.3 %copy-start.25 = (bf16[12,64,128]{2,1,0:T(8,128)(2,1)}, bf16[12,64,128]{2,1,0:T(8,128)(2,1)S(1)}, u32[]{:S(2)}) copy-start(bf16[12,64,128]{2,1,0:T(8,128)(2,1)S(1)} %convolution_convert_fusion.12) | copy-start | bytes 589828
  203.0 3.7 copy-start.47
  203.2 3.5 copy-start.31
  209.1 15.7 %copy-start.19 = (f32[128,768]{1,0:T(8,128)}, f32[128,768]{1,0:T(8,128)S(1)}, u32[]{:S(2)}) copy-start(f32[128,768]{1,0:T(8,128)S(1)} %get-tuple-element.94) | copy-start | bytes 1179652
  219.3 1.9 copy-start.22
  219.3 1.9 copy-start.49
  221.3 1.6 copy-start.60
  222.9 1.9 copy-start.56
  222.9 1.9 copy-start.58
  222.9 2.1 copy-start.18
  222.9 2.1 copy-start.40
  225.5 3.9 copy-start.17
  225.5 3.9 copy-start.26
  226.4 2.8 copy-start.42
  226.6 2.6 copy-start.51
  226.6 3.7 copy-start.38
  229.4 14.5 %copy-start.2 = (f32[128,768]{1,0:T(8,128)}, f32[128,768]{1,0:T(8,128)S(1)}, u32[]{:S(2)}) copy-start(f32[128,768]{1,0:T(8,128)S(1)} %multiply_add_fusion.3) | copy-start | bytes 1179652
  229.4 2.2 copy-start.34
  229.9 1.9 copy-start.54
  229.9 4.0 copy-start.30
  229.9 4.0 copy-start.43
  239.3 2.9 copy-start.52
  239.3 4.5 copy-start.27
  239.3 6.0 %copy-start.41 = (bf16[12,64,128]{2,1,0:T(8,128)(2,1)S(1)}, bf16[12,64,128]{2,1,0:T(8,128)(2,1)}, u32[]{:S(2)}) copy-start(bf16[12,64,128]{2,1,0:T(8,128)(2,1)} %copy-done.39) | copy-start | bytes 589828
  242.2 4.6 copy-start.20
  242.2 4.6 copy-start.57
  242.2 4.6 copy-start.59
  251.2 2.3 copy-start.61
  269.0 4.9 copy-start.64
  273.9 2.4 copy-start.24
  274.7 2.7 copy-start.23
  292.0 2.5 copy-start.9
  292.0 3.6 copy-start.12
  292.0 4.8 copy-start.16
  294.5 3.4 copy-start.15
  295.6 3.5 copy-start.11
  296.7 3.5 copy-start.10
  297.9 3.4 copy-start.8
  299.1 3.5 copy-start.7
  300.2 3.5 copy-start.14
  301.4 3.5 copy-start.6
  302.5 3.4 copy-start.5
  303.7 3.4 copy-start.13
  308.2 1.9 copy-start.46
  308.2 2.8 copy-start.66
  311.9 2.8 copy-start.21
  311.9 2.8 copy-start.62
  312.0 6.7 %copy-start.67 = (f32[128]{0:T(128)S(1)}, f32[128]{0:T(128)}, u32[]{:S(2)}) copy-start(f32[128]{0:T(128)} %get-tuple-element.49) | copy-start | bytes 1540
  312.0 10.1 %copy-start.3 = (f32[128,768]{1,0:T(8,128)S(1)}, f32[128,768]{1,0:T(8,128)}, u32[]{:S(2)}) copy-start(f32[128,768]{1,0:T(8,128)} %copy-done.2) | copy-start | bytes 1179652
  312.0 10.1 %copy-start.63 = (f32[128,768]{1,0:T(8,128)S(1)}, f32[128,768]{1,0:T(8,128)}, u32[]{:S(2)}) copy-start(f32[128,768]{1,0:T(8,128)} %get-tuple-element.101) | copy-start | bytes 1179652
  312.0 1.2 collective-permute-start
  313.3 13.6 %copy-start.65 = (bf16[1,64,768]{2,1,0:T(8,128)(2,1)S(1)}, bf16[1,64,768]{2,1,0:T(8,128)(2,1)}, u32[]{:S(2)}) copy-start(bf16[1,64,768]{2,1,0:T(8,128)(2,1)} %copy.124) | copy-start | bytes 294916
  313.3 5.2 collective-permute-start.1
  318.5 3.7 collective-permute-start.2
  322.1 3.7 collective-permute-start.3
  325.8 4.5 collective-permute-start.4
  524.0 2.0 copy-start.28
  (11 other events, 13.0 us)
Sparse Core Ops, SparseCore 0:
  16.6 132.1 all-gather.2
  312.1 211.8 reduce-scatter.1
